TPU v7x, 32 devices: a whole 2x2x4 slice. The times are simulated.
32 devices in a mesh: dp: 8 (over y, x, core), tp: 4 (over z).
Axes of the slice: x: 2, y: 2, z: 4, core: 2. Of those that a mesh axis runs over, the one named last changes fastest.
Arguments:
- layer_in: bfloat16 [32768, 768], P(('dp', 'tp')), may hold values from -6 to 6
- out_grad: bfloat16 [32768, 768], P(('dp', 'tp')), may hold values from -6 to 6
- lengths: int32 [8], P('dp'), may hold values from 2049 to 4096, as said below
- w_query: bfloat16 [768, 768], replicated, may hold values from -0.875 to 0.875
- b_query: bfloat16 [768], replicated, may hold values from -6 to 6
- w_key: bfloat16 [768, 768], replicated, may hold values from -0.21875 to 0.21875
- b_key: bfloat16 [768], replicated, may hold values from -3 to 3
- w_value: bfloat16 [768, 768], replicated, may hold values from -0.21875 to 0.21875
- b_value: bfloat16 [768], replicated, may hold values from -3 to 3
- w_out: bfloat16 [768, 768], replicated, may hold values from -0.875 to 0.875
- b_out: bfloat16 [768], replicated, may hold values from -3 to 3
- seq_proj: bfloat16 [256, 4096], replicated, may hold values from -0.09375 to 0.09375
- attn_gain: bfloat16 [768], replicated, may hold values from 0.5 to 1.5
- attn_shift: bfloat16 [768], replicated, may hold values from -3 to 3
- w_up: bfloat16 [768, 3072], P(None, 'tp'), may hold values from -0.21875 to 0.21875
- b_up: bfloat16 [3072], P('tp'), may hold values from -3 to 3
- w_down: bfloat16 [3072, 768], P('tp'), may hold values from -0.109375 to 0.109375
- b_down: bfloat16 [768], replicated, may hold values from -3 to 3
- ffn_gain: bfloat16 [768], replicated, may hold values from 0.5 to 1.5
- ffn_shift: bfloat16 [768], replicated, may hold values from -3 to 3
Outputs:
- layer_out: bfloat16 [32768, 768], P(('dp', 'tp'))
- grad_in: bfloat16 [32768, 768], P(('dp', 'tp'))
- grad_w_query: float32 [768, 768], replicated
- grad_b_query: float32 [768], replicated
- grad_w_key: float32 [768, 768], replicated
- grad_b_key: float32 [768], replicated
- grad_w_value: float32 [768, 768], replicated
- grad_b_value: float32 [768], replicated
- grad_w_out: float32 [768, 768], replicated
- grad_b_out: float32 [768], replicated
- grad_seq_proj: float32 [256, 4096], replicated
- grad_attn_gain: float32 [768], replicated
- grad_attn_shift: float32 [768], replicated
- grad_w_up: float32 [768, 3072], P(None, 'tp')
- grad_b_up: float32 [3072], P('tp')
- grad_w_down: float32 [3072, 768], P('tp')
- grad_b_down: float32 [768], replicated
- grad_ffn_gain: float32 [768], replicated
- grad_ffn_shift: float32 [768], replicated
Inputs may be any that keep to these rules, and one draw needn't show every extreme that they name: `lengths`: rows from a sequence's length on are padding; some sequence has exactly 4096 rows.
All inputs are finite; a program needn't handle non-finite values.
Results may differ from a plain program's by a relative error of at most 0.022.
The roundings to bfloat16 on the way count: a program that leaves them out, or rounds other values in their place, can miss the bound.
Values may be sent and summed in bfloat16 or wider, within the bound.
A program may use at most 192 MiB of HBM per device.

v0:
```python
import jax
import jax.numpy as jnp
from jax import lax
from jax.sharding import PartitionSpec as P

HEADS = 12
HEAD = 64


def layer_norm(hidden, gain, shift):
    center = hidden - jnp.mean(hidden, axis=-1, keepdims=True)
    spread = jnp.mean(center * center, axis=-1, keepdims=True)
    return center * lax.rsqrt(spread + 1e-05) * gain + shift


def matmul(left, right):
    return jnp.dot(left, right, preferred_element_type=jnp.float32)


def contract_rows(left, right):
    return lax.dot_general(
        left, right, (((0,), (0,)), ((), ())), preferred_element_type=jnp.float32
    )


def times_transpose(left, right):
    return lax.dot_general(
        left, right, (((1,), (1,)), ((), ())), preferred_element_type=jnp.float32
    )


def exact_gelu(value):
    return jax.nn.gelu(value, approximate=False)


def on_device(
    layer_in,
    out_grad,
    lengths,
    w_query,
    b_query,
    w_key,
    b_key,
    w_value,
    b_value,
    w_out,
    b_out,
    seq_proj,
    attn_gain,
    attn_shift,
    w_up,
    b_up,
    w_down,
    b_down,
    ffn_gain,
    ffn_shift,
):
    row_count = layer_in.shape[0]
    width = layer_in.shape[1]
    slots = seq_proj.shape[0]
    tp_parts = lax.axis_size("tp")
    tp_index = lax.axis_index("tp")
    total_rows = row_count * tp_parts
    own_first = tp_index * row_count
    own_positions = own_first + jnp.arange(row_count, dtype=jnp.int32)
    own_live = (own_positions < lengths[0]).astype(jnp.float32)
    own_keys = (matmul(layer_in, w_key) + b_key.astype(jnp.float32)).astype(jnp.bfloat16)
    own_values = (matmul(layer_in, w_value) + b_value.astype(jnp.float32)).astype(jnp.bfloat16)
    own_cols = lax.dynamic_slice_in_dim(seq_proj, own_first, row_count, 1)
    own_proj = (own_cols.astype(jnp.float32) * own_live[None, :]).astype(jnp.bfloat16)
    share_keys = matmul(own_proj, own_keys)
    share_values = matmul(own_proj, own_values)
    proj_keys, proj_values = lax.psum((share_keys, share_values), "tp")
    proj_keys = proj_keys.astype(jnp.bfloat16)
    proj_values = proj_values.astype(jnp.bfloat16)
    queries = (matmul(layer_in, w_query) + b_query.astype(jnp.float32)).astype(jnp.bfloat16)
    block_rows = min(512, row_count)
    block_count = row_count // block_rows
    query_blocks = queries.reshape(block_count, block_rows, HEADS, HEAD)
    key_heads = proj_keys.reshape(slots, HEADS, HEAD)
    value_heads = proj_values.reshape(slots, HEADS, HEAD)

    def attend(query_block):
        logits = (
            jnp.einsum("rhd,khd->rhk", query_block, key_heads, preferred_element_type=jnp.float32)
            * 0.125
        )
        summit = jax.scipy.special.logsumexp(logits, axis=-1)
        weights_b = jnp.exp(logits - summit[..., None]).astype(jnp.bfloat16)
        result = jnp.einsum(
            "rhk,khd->rhd", weights_b, value_heads, preferred_element_type=jnp.float32
        )
        return (result.astype(jnp.bfloat16), summit)

    mixed_blocks, summits = lax.map(attend, query_blocks)
    mixed = mixed_blocks.reshape(row_count, width)
    attn = matmul(mixed, w_out) + b_out.astype(jnp.float32)
    res_one = layer_in.astype(jnp.float32) + attn
    normed, norm_one_pull = jax.vjp(
        layer_norm, res_one, attn_gain.astype(jnp.float32), attn_shift.astype(jnp.float32)
    )
    normed_b = normed.astype(jnp.bfloat16)
    ffn_rows = lax.all_gather(normed_b, "tp", axis=0, tiled=True)
    pre_act = matmul(ffn_rows, w_up) + b_up.astype(jnp.float32)
    hidden_act, gelu_pull = jax.vjp(exact_gelu, pre_act)
    hidden_b = hidden_act.astype(jnp.bfloat16)
    branch = lax.psum_scatter(
        matmul(hidden_b, w_down).astype(jnp.bfloat16), "tp", scatter_dimension=0, tiled=True
    ).astype(jnp.float32)
    branch = branch + b_down.astype(jnp.float32)
    res_two = normed + branch
    final, norm_two_pull = jax.vjp(
        layer_norm, res_two, ffn_gain.astype(jnp.float32), ffn_shift.astype(jnp.float32)
    )
    layer_out = final.astype(jnp.bfloat16)
    d_res_two, g_ffn_gain, g_ffn_shift = norm_two_pull(out_grad.astype(jnp.float32))
    d_branch = d_res_two.astype(jnp.bfloat16)
    g_b_down = jnp.sum(d_branch.astype(jnp.float32), axis=0)
    d_rows = lax.all_gather(d_branch, "tp", axis=0, tiled=True)
    g_w_down = contract_rows(hidden_b, d_rows)
    (d_hidden,) = gelu_pull(times_transpose(d_rows, w_down))
    d_pre = d_hidden.astype(jnp.bfloat16)
    g_b_up = jnp.sum(d_pre.astype(jnp.float32), axis=0)
    g_w_up = contract_rows(ffn_rows, d_pre)
    d_normed_ffn = lax.psum_scatter(
        times_transpose(d_pre, w_up).astype(jnp.bfloat16), "tp", scatter_dimension=0, tiled=True
    ).astype(jnp.float32)
    d_normed = d_res_two + d_normed_ffn
    d_res_one, g_attn_gain, g_attn_shift = norm_one_pull(d_normed)
    d_attn = d_res_one.astype(jnp.bfloat16)
    g_b_out = jnp.sum(d_attn.astype(jnp.float32), axis=0)
    g_w_out = contract_rows(mixed, d_attn)
    d_mixed = times_transpose(d_attn, w_out).astype(jnp.bfloat16)
    d_mixed_blocks = d_mixed.reshape(block_count, block_rows, HEADS, HEAD)

    def attend_back(running, element):
        key_total, value_total = running
        query_block, summit, d_block = element
        logits = (
            jnp.einsum("rhd,khd->rhk", query_block, key_heads, preferred_element_type=jnp.float32)
            * 0.125
        )
        probs = jnp.exp(logits - summit[..., None])
        probs_b = probs.astype(jnp.bfloat16)
        d_probs = jnp.einsum(
            "rhd,khd->rhk", d_block, value_heads, preferred_element_type=jnp.float32
        )
        d_logits = (probs * (d_probs - jnp.sum(probs * d_probs, axis=-1, keepdims=True))).astype(
            jnp.bfloat16
        )
        d_query = (
            jnp.einsum("rhk,khd->rhd", d_logits, key_heads, preferred_element_type=jnp.float32)
            * 0.125
        )
        key_total = (
            key_total
            + jnp.einsum("rhk,rhd->khd", d_logits, query_block, preferred_element_type=jnp.float32)
            * 0.125
        )
        value_total = value_total + jnp.einsum(
            "rhk,rhd->khd", probs_b, d_block, preferred_element_type=jnp.float32
        )
        return ((key_total, value_total), d_query.astype(jnp.bfloat16))

    zero_heads = jnp.zeros((slots, HEADS, HEAD), jnp.float32)
    (key_part, value_part), d_query_blocks = lax.scan(
        attend_back, (zero_heads, zero_heads), (query_blocks, summits, d_mixed_blocks)
    )
    d_queries = d_query_blocks.reshape(row_count, width)
    d_proj_keys, d_proj_values = (
        lax.psum(key_part.reshape(slots, width).astype(jnp.bfloat16), "tp").astype(jnp.float32),
        lax.psum(value_part.reshape(slots, width).astype(jnp.bfloat16), "tp").astype(jnp.float32),
    )
    d_proj_keys = d_proj_keys.astype(jnp.bfloat16)
    d_proj_values = d_proj_values.astype(jnp.bfloat16)
    d_keys = contract_rows(own_proj, d_proj_keys).astype(jnp.bfloat16)
    d_values = contract_rows(own_proj, d_proj_values).astype(jnp.bfloat16)
    own_proj_grad = (
        times_transpose(d_proj_keys, own_keys) + times_transpose(d_proj_values, own_values)
    ) * own_live[None, :]
    g_seq_proj = lax.dynamic_update_slice_in_dim(
        jnp.zeros((slots, total_rows), jnp.float32), own_proj_grad, own_first, 1
    )
    g_w_query = contract_rows(layer_in, d_queries)
    g_b_query = jnp.sum(d_queries.astype(jnp.float32), axis=0)
    g_w_key = contract_rows(layer_in, d_keys)
    g_b_key = jnp.sum(d_keys.astype(jnp.float32), axis=0)
    g_w_value = contract_rows(layer_in, d_values)
    g_b_value = jnp.sum(d_values.astype(jnp.float32), axis=0)
    grad_in = (
        d_res_one
        + times_transpose(d_queries, w_query)
        + times_transpose(d_keys, w_key)
        + times_transpose(d_values, w_value)
    ).astype(jnp.bfloat16)
    (
        g_w_query,
        g_w_key,
        g_w_value,
        g_w_out,
        g_seq_proj,
        g_b_query,
        g_b_key,
        g_b_value,
        g_b_out,
        g_attn_gain,
        g_attn_shift,
        g_ffn_gain,
        g_ffn_shift,
        g_b_down,
    ) = lax.psum(
        (
            g_w_query,
            g_w_key,
            g_w_value,
            g_w_out,
            g_seq_proj,
            g_b_query,
            g_b_key,
            g_b_value,
            g_b_out,
            g_attn_gain,
            g_attn_shift,
            g_ffn_gain,
            g_ffn_shift,
            g_b_down,
        ),
        ("dp", "tp"),
    )
    g_w_up, g_b_up, g_w_down = lax.psum((g_w_up, g_b_up, g_w_down), "dp")
    return (
        layer_out,
        grad_in,
        g_w_query,
        g_b_query,
        g_w_key,
        g_b_key,
        g_w_value,
        g_b_value,
        g_w_out,
        g_b_out,
        g_seq_proj,
        g_attn_gain,
        g_attn_shift,
        g_w_up,
        g_b_up,
        g_w_down,
        g_b_down,
        g_ffn_gain,
        g_ffn_shift,
    )


def solution(mesh):
    in_specs = (
        P(("dp", "tp"), None),
        P(("dp", "tp"), None),
        P("dp"),
        P(),
        P(),
        P(),
        P(),
        P(),
        P(),
        P(),
        P(),
        P(),
        P(),
        P(),
        P(None, "tp"),
        P("tp"),
        P("tp", None),
        P(),
        P(),
        P(),
    )
    out_specs = (
        P(("dp", "tp"), None),
        P(("dp", "tp"), None),
        P(),
        P(),
        P(),
        P(),
        P(),
        P(),
        P(),
        P(),
        P(),
        P(),
        P(),
        P(None, "tp"),
        P("tp"),
        P("tp", None),
        P(),
        P(),
        P(),
    )
    return jax.shard_map(
        on_device, mesh=mesh, in_specs=in_specs, out_specs=out_specs, check_vma=False
    )
```

profile of v0, /device:TPU:0, one launch (start us, length us, event | category | flops | bytes accessed | tf_op | source)
XLA Modules:
  0.0 1117.3 jit_solution(10581152237849772163)
XLA Ops:
  18.0 62.3 %all-reduce.15 = (bf16[256,768]{1,0:T(8,128)(2,1)S(1)}, bf16[256,768]{1,0:T(8,128)(2,1)}) all-reduce(f32[256,768]{1,0:T(8,128)S(1)} %fusion.73, f32[256,768]{1,0:T(8,128)S(1)} %fusion.72), channel_id=1, replica_groups=mesh['dp'=8,'tp'=4] {'tp'}, use_global_device_ids=true, to_apply=%region_0.0 | all-reduce | flops 393216 | bytes 2359296 | tf_op jit(solution)/shard_map/psum | solution.py:73
  81.7 4.3 add_convert_fusion.5
  93.1 9.8 while.27
  102.9 3.9 copy.71
  112.9 113.9 %all-gather.3.cloned.1.call-done = bf16[4096,768]{0,1:T(8,128)(2,1)} async-done(((bf16[1024,768]{0,1:T(8,128)(2,1)}), bf16[4096,768]{0,1:T(8,128)(2,1)}) %all-gather.3.cloned.1.call-update) | async-done | bytes 6291472 | tf_op jit(solution)/shard_map/all_gather | solution.py:103
  226.8 34.7 %multiply_convert_fusion.1 = (bf16[4096,768]{1,0:T(8,128)(2,1)S(1)}, f32[4096,768]{1,0:T(8,128)}, f32[4096,768]{1,0:T(8,128)}) fusion(f32[768]{0:T(1024)S(1)} %convert_element_type.178, bf16[4096,768]{0,1:T(8,128)(2,1)} %all-gather.3.cloned.1.call-done, bf16[768,768]{1,0:T(8,128)(2,1)S(1)} %copy-done), kind=kOutput, calls=%fused_computation.63 | convolution fusion | flops 5039456256 | bytes 38931456 | tf_op jit(solution)/shard_map/dot_general | solution.py:17
  264.2 7.0 convolution_convert_fusion.1
  273.7 106.7 %reduce-scatter.3.cloned.1.call-done = bf16[1024,768]{0,1:T(8,128)(2,1)} async-done(((bf16[4096,768]{0,1:T(8,128)(2,1)}), bf16[1024,768]{0,1:T(8,128)(2,1)}) %reduce-scatter.3.cloned.1.call-update) | async-done | bytes 1572880 | tf_op jit(solution)/shard_map/reduce_scatter | solution.py:107
  380.3 3.2 fusion.84
  392.1 116.0 %all-gather.5.cloned.1.call-done = bf16[4096,768]{0,1:T(8,128)(2,1)} async-done(((bf16[1024,768]{0,1:T(8,128)(2,1)}), bf16[4096,768]{0,1:T(8,128)(2,1)}) %all-gather.5.cloned.1.call-update) | async-done | bytes 6291472 | tf_op jit(solution)/shard_map/all_gather | solution.py:119
  508.1 18.6 %convert_reduce_fusion = (f32[768]{0:T(1024)}, bf16[4096,768]{1,0:T(8,128)(2,1)}) fusion(f32[4096,768]{1,0:T(8,128)} %get-tuple-element.273, f32[4096,768]{1,0:T(8,128)} %get-tuple-element.281, f32[768]{0:T(1024)S(1)} %convert_element_type.178, bf16[4096,768]{0,1:T(8,128)(2,1)} %all-gather.5.cloned.1.call-done, bf16[768,768]{1,0:T(8,128)(2,1)S(1)} %copy-done.66), kind=kOutput, calls=%fused_computation.61 | convolution fusion | flops 4885314560 | bytes 38934528 | tf_op jit(solution)/shard_map/dot_general | solution.py:27
  526.7 9.8 convolution_convert_fusion
  536.7 108.8 %reduce-scatter.5.cloned.1.call-done = bf16[1024,768]{0,1:T(8,128)(2,1)} async-done(((bf16[4096,768]{0,1:T(8,128)(2,1)}), bf16[1024,768]{0,1:T(8,128)(2,1)}) %reduce-scatter.5.cloned.1.call-update) | async-done | bytes 1572880 | tf_op jit(solution)/shard_map/reduce_scatter | solution.py:125
  645.5 5.4 multiply_reduce_fusion
  662.1 3.0 copy.77
  666.5 33.9 %while.28 = (s32[]{:T(128)}, f32[256,12,64]{0,2,1:T(8,128)}, f32[256,12,64]{0,2,1:T(8,128)S(1)}, bf16[2,512,12,64]{1,3,2,0:T(8,128)(2,1)}, bf16[2,512,12,64]{1,3...) while((s32[]{:T(128)}, f32[256,12,64]{0,2,1:T(8,128)}, ...), condition=%wide.region_18.19_spmd.clone, body=%wide.region_16.18_spmd.clone.sunk | while | flops 1027270656 | bytes 112255784 | solution.py:166
  675.3 4.0 fusion.185
  679.3 4.1 fusion.186
  692.2 4.1 fusion.185
  696.3 4.1 fusion.186
  711.2 36.7 %all-reduce.14.cloned.1.call-done = (bf16[256,768]{0,1:T(8,128)(2,1)}, bf16[256,768]{0,1:T(8,128)(2,1)}) async-done(((bf16[256,768]{0,1:T(8,128)(2,1)}, bf16[256,768]{0,1:T(8,128)(2,1)}), (bf16[256,768]{0,1:T(8,128)(2,1)}, bf16[256,768]{0,1:T(8,128)(2,1)})) %all-reduce.14.cloned.1.call-update) | async-done | bytes 786448 | tf_op jit(solution)/shard_map/psum | solution.py:172
  753.6 2.9 convolution_bitcast_fusion.1
  756.5 2.9 convolution_bitcast_fusion
  763.8 10.1 fusion.92
  773.9 10.2 fusion.91
  786.9 14.2 %psum.163 = f32[768]{0:T(1024)} all-reduce(f32[768]{0:T(1024)S(1)} %copy-done.55), channel_id=1, replica_groups=mesh['dp'=8,'tp'=4] {'dp'}, use_global_device_ids=true, to_apply=%region_40.41 | all-reduce | flops 768 | bytes 6144 | tf_op jit(solution)/shard_map/psum | solution.py:230
  801.4 3.1 fusion.87
  810.8 40.6 %all-reduce = (f32[768]{0:T(1024)}, f32[768]{0:T(1024)}, f32[768]{0:T(1024)}, f32[768]{0:T(1024)}, f32[768]{0:T(1024)}, /*index=5*/f32[768]{0:T(1024)}, f32[768]{0:T(1024)}, f32[768]{0:T(1024)}, f32[768]{0:T(1024)}) all-reduce(f32[768]{0:T(1024)S(1)} %reduce_sum.197, ...), channel_id=1, replica_groups=mesh['dp'=8,'tp'=4] {'dp','tp'}, use_global_device_ids=true, to_apply=%region_23.24 | all-reduce | flops 6912 | bytes 55296 | tf_op jit(solution)/shard_map/psum | solution.py:211
  851.4 157.9 %all-reduce.10.cloned.1.call-done = (f32[768,768]{0,1:T(8,128)}, f32[768,768]{0,1:T(8,128)}, f32[768,768]{0,1:T(8,128)}, f32[768,768]{1,0:T(8,128)}, f32[256,4096]{1,0:T(8,128)}) async-done(((f32[768,768]{0,1:T(8,128)}, f32[768,768]{0,1:T(8,128)}, f32[768,768]{0,1:T(8,128)}, f32[768,768]{1,0:T(8,128)}, f32[256,4096]{1,0:T(8,128)}), (f32[768,768]{0,1:T(8,128)}, f32[768,768]{0,1:T(8,128)}, ...) | async-done | bytes 13631504 | tf_op jit(solution)/shard_map/psum | solution.py:211
  1009.3 3.2 copy.84
  1014.4 3.2 copy.86
  1017.6 82.2 %all-reduce.12.cloned.1.call-done = (f32[768,768]{1,0:T(8,128)}, f32[768,768]{1,0:T(8,128)}) async-done(((f32[768,768]{1,0:T(8,128)}, f32[768,768]{1,0:T(8,128)}), (f32[768,768]{1,0:T(8,128)}, f32[768,768]{1,0:T(8,128)})) %all-reduce.12.cloned.1.call-update) | async-done | bytes 4718608 | tf_op jit(solution)/shard_map/psum | solution.py:230
  (272 shorter events, 119.7 us)
Async XLA Ops:
  7.2 219.6 %copy-start = (bf16[768,768]{1,0:T(8,128)(2,1)S(1)}, bf16[768,768]{1,0:T(8,128)(2,1)}, u32[]{:S(2)}) copy-start(bf16[768,768]{1,0:T(8,128)(2,1)} %param.38) | copy-start | bytes 3538948
  7.2 4.2 copy-start.32
  7.2 219.6 %all-gather.3.cloned.1.call-start = ((), (), s32[]{:S(2)}) async-start(), calls=%async_computation.2 | async-start | bytes 7864320 | tf_op jit(solution)/shard_map/all_gather | solution.py:103
  8.1 8.2 copy-start.46
  17.4 64.2 %copy-start.57 = (bf16[768]{0:T(1024)(128)(2,1)S(1)}, bf16[768]{0:T(1024)(128)(2,1)}, u32[]{:S(2)}) copy-start(bf16[768]{0:T(1024)(128)(2,1)} %param.28) | copy-start | bytes 4612
  102.9 4.4 copy-start.4
  102.9 4.4 copy-start.7
  102.9 4.4 copy-start.15
  102.9 4.4 copy-start.58
  102.9 4.4 copy-start.37
  102.9 4.4 copy-start.67
  112.4 268.0 %reduce-scatter.3.cloned.1.call-start = ((), (), s32[]{:S(2)}) async-start(), calls=%async_computation.3 | async-start | bytes 7864320 | tf_op jit(solution)/shard_map/reduce_scatter | solution.py:107
  112.9 151.3 %copy-start.65 = (bf16[768,768]{1,0:T(8,128)(2,1)S(1)}, bf16[768,768]{1,0:T(8,128)(2,1)}, u32[]{:S(2)}) copy-start(bf16[768,768]{1,0:T(8,128)(2,1)} %param.40) | copy-start | bytes 3538948
  271.3 236.8 %all-gather.5.cloned.1.call-start = ((), (), s32[]{:S(2)}) async-start(), calls=%async_computation.4 | async-start | bytes 7864320 | tf_op jit(solution)/shard_map/all_gather | solution.py:119
  390.0 118.1 %copy-start.66 = (bf16[768,768]{1,0:T(8,128)(2,1)S(1)}, bf16[768,768]{1,0:T(8,128)(2,1)}, u32[]{:S(2)}) copy-start(bf16[768,768]{1,0:T(8,128)(2,1)} %param.40) | copy-start | bytes 3538948
  392.1 253.5 %reduce-scatter.5.cloned.1.call-start = ((), (), s32[]{:S(2)}) async-start(), calls=%async_computation.5 | async-start | bytes 7864320 | tf_op jit(solution)/shard_map/reduce_scatter | solution.py:125
  536.5 211.4 %all-reduce.14.cloned.1.call-start = ((), (), s32[]{:S(2)}) async-start(), calls=%async_computation.8 | async-start | bytes 1572864 | tf_op jit(solution)/shard_map/psum | solution.py:172
  536.7 114.3 %copy-start.49 = (f32[1024]{0:T(1024)S(1)}, f32[1024]{0:T(1024)}, u32[]{:S(2)}) copy-start(f32[1024]{0:T(1024)} %copy-done.48) | copy-start | bytes 12292
  645.5 5.5 copy-start.10
  645.5 5.5 copy-start.14
  645.5 5.6 copy-start.26
  662.1 4.4 copy-start.5
  662.1 4.4 copy-start.8
  662.1 4.4 copy-start.16
  662.1 4.4 copy-start.44
  692.2 4.2 copy-start.12
  703.1 306.1 %all-reduce.10.cloned.1.call-start = ((), (), s32[]{:S(2)}) async-start(), calls=%async_computation.6 | async-start | bytes 27262976 | tf_op jit(solution)/shard_map/psum | solution.py:211
  708.4 39.5 %copy-start.47 = (f32[1024]{0:T(1024)S(1)}, f32[1024]{0:T(1024)}, u32[]{:S(2)}) copy-start(f32[1024]{0:T(1024)} %copy-done.46) | copy-start | bytes 12292
  749.8 6.6 copy-start.72
  763.5 336.4 %all-reduce.12.cloned.1.call-start = ((), (), s32[]{:S(2)}) async-start(), calls=%async_computation.7 | async-start | bytes 9437184 | tf_op jit(solution)/shard_map/psum | solution.py:230
  784.2 17.3 %copy-start.70 = (bf16[768,768]{1,0:T(8,128)(2,1)S(1)}, bf16[768,768]{1,0:T(8,128)(2,1)}, u32[]{:S(2)}) copy-start(bf16[768,768]{1,0:T(8,128)(2,1)} %param.29) | copy-start | bytes 3538948
  1014.4 85.4 %copy-start.28 = (f32[768,768]{1,0:T(8,128)S(1)}, f32[768,768]{1,0:T(8,128)}, u32[]{:S(2)}) copy-start(f32[768,768]{1,0:T(8,128)} %get-tuple-element.448) | copy-start | bytes 7077892
  (58 other events, 132.1 us)
Sparse Core Ops, SparseCore 0:
  112.5 114.2 all-gather.2
  271.4 108.9 reduce-scatter.2
  392.2 115.8 all-gather.4
  536.6 108.9 reduce-scatter.4
  703.3 44.5 all-reduce.13
  763.6 245.6 all-reduce.9
  1013.0 86.8 all-reduce.11
where the time goes:
time: 1120 us
  waiting for transfers between devices  722 us (64%)
  matrix products  160 us (14%)
  blocking collectives  117 us (10%)
  local copies, waits for them, and re-layouts  70.9 us (6%)
  other arithmetic  28.8 us (3%)
  between operations  16.3 us (1%)
    psum x1, waiting for transfers between devices, on_device(): lax.psum((g_w_query, g_w_key, g_w_value, g_w_out, g_seq_proj, g_b_query,...  158 us
    all_gather x1, waiting for transfers between devices, on_device(): d_rows = lax.all_gather(d_branch, 'tp', axis=0, tiled=True)  116 us
    all_gather x1, waiting for transfers between devices, on_device(): ffn_rows = lax.all_gather(normed_b, 'tp', axis=0, tiled=True)  114 us
    reduce_scatter x1, waiting for transfers between devices, on_device(): lax.psum_scatter(times_transpose(d_pre, w_up).astype(jnp.bfloat16), 'tp',...  109 us
    reduce_scatter x1, waiting for transfers between devices, on_device(): lax.psum_scatter(matmul(hidden_b, w_down).astype(jnp.bfloat16), 'tp', sca...  107 us
    psum x1, waiting for transfers between devices, on_device(): g_w_up, g_b_up, g_w_down = lax.psum((g_w_up, g_b_up, g_w_down), 'dp')  82.2 us
    psum x1, blocking collectives, on_device(): proj_keys, proj_values = lax.psum((share_keys, share_values), 'tp')  62.3 us
    dot_general x8, matrix products, matmul(): return jnp.dot(left, right, preferred_element_type=jnp.float32)  53 us
  transfers between devices with their start and end apart: 7, of which 7 were waited for; matrix products, arithmetic and copies ran while one was open for 4% of the time, Pallas kernels for 0%

commit v1 on v0

--- a/solution.py
+++ b/solution.py
@@ -209,23 +209,26 @@
         g_ffn_shift,
         g_b_down,
     ) = lax.psum(
-        (
-            g_w_query,
-            g_w_key,
-            g_w_value,
-            g_w_out,
-            g_seq_proj,
-            g_b_query,
-            g_b_key,
-            g_b_value,
-            g_b_out,
-            g_attn_gain,
-            g_attn_shift,
-            g_ffn_gain,
-            g_ffn_shift,
-            g_b_down,
+        lax.psum(
+            (
+                g_w_query,
+                g_w_key,
+                g_w_value,
+                g_w_out,
+                g_seq_proj,
+                g_b_query,
+                g_b_key,
+                g_b_value,
+                g_b_out,
+                g_attn_gain,
+                g_attn_shift,
+                g_ffn_gain,
+                g_ffn_shift,
+                g_b_down,
+            ),
+            "tp",
         ),
-        ("dp", "tp"),
+        "dp",
     )
     g_w_up, g_b_up, g_w_down = lax.psum((g_w_up, g_b_up, g_w_down), "dp")
     return (

time: 1120 us -> 1500 us (1.34)
  waiting for transfers between devices: 722 us -> 1110 us
    psum x1, waiting for transfers between devices: 158 us -> 442 us  [on_device(): lax.psum((g_w_query, g_w_key, g_w_value, g_w_out, g_seq_proj, g_b_query,...]
    psum x1, waiting for transfers between devices: 82.2 us -> 190 us  [on_device(): lax.psum(lax.psum((g_w_query, g_w_key, g_w_value, g_w_out, g_seq_proj, g_...]
    psum x1, blocking collectives: 40.6 us -> 17 us  [on_device(): lax.psum((g_w_query, g_w_key, g_w_value, g_w_out, g_seq_proj, g_b_query,...]
    unnamed x152 -> x154, local copies, waits for them, and re-layouts: 43 us -> 42.4 us
  transfers between devices with their start and end apart: 7 -> 7, of which waited for: 7 -> 7; matrix products, arithmetic and copies ran while one was open for 4% -> 3% of each run, Pallas kernels for 0% -> 0%
where the time goes in v1:
time: 1500 us
  waiting for transfers between devices  1110 us (74%)
  matrix products  160 us (11%)
  blocking collectives  105 us (7%)
  local copies, waits for them, and re-layouts  70.3 us (5%)
  other arithmetic  29.4 us (2%)
  between operations  16.1 us (1%)
    psum x1, waiting for transfers between devices, on_device(): lax.psum((g_w_query, g_w_key, g_w_value, g_w_out, g_seq_proj, g_b_query,...  442 us
    psum x1, waiting for transfers between devices, on_device(): lax.psum(lax.psum((g_w_query, g_w_key, g_w_value, g_w_out, g_seq_proj, g_...  190 us
    all_gather x1, waiting for transfers between devices, on_device(): d_rows = lax.all_gather(d_branch, 'tp', axis=0, tiled=True)  116 us
    all_gather x1, waiting for transfers between devices, on_device(): ffn_rows = lax.all_gather(normed_b, 'tp', axis=0, tiled=True)  114 us
    reduce_scatter x1, waiting for transfers between devices, on_device(): lax.psum_scatter(times_transpose(d_pre, w_up).astype(jnp.bfloat16), 'tp',...  109 us
    reduce_scatter x1, waiting for transfers between devices, on_device(): lax.psum_scatter(matmul(hidden_b, w_down).astype(jnp.bfloat16), 'tp', sca...  107 us
    psum x1, blocking collectives, on_device(): proj_keys, proj_values = lax.psum((share_keys, share_values), 'tp')  62.3 us
    dot_general x8, matrix products, matmul(): return jnp.dot(left, right, preferred_element_type=jnp.float32)  53 us
  transfers between devices with their start and end apart: 7, of which 7 were waited for; matrix products, arithmetic and copies ran while one was open for 3% of the time, Pallas kernels for 0%

profile of v1, /device:TPU:0, one launch (start us, length us, event | category | flops | bytes accessed | tf_op | source)
XLA Modules:
  0.0 1495.5 jit_solution(6238773219830605769)
XLA Ops:
  18.0 62.3 %all-reduce.16 = (bf16[256,768]{1,0:T(8,128)(2,1)S(1)}, bf16[256,768]{1,0:T(8,128)(2,1)}) all-reduce(f32[256,768]{1,0:T(8,128)S(1)} %fusion.73, f32[256,768]{1,0:T(8,128)S(1)} %fusion.72), channel_id=1, replica_groups=mesh['dp'=8,'tp'=4] {'tp'}, use_global_device_ids=true, to_apply=%region_0.0 | all-reduce | flops 393216 | bytes 2359296 | tf_op jit(solution)/shard_map/psum | solution.py:73
  81.6 4.3 add_convert_fusion.5
  93.0 9.8 while.27
  102.9 3.9 copy.71
  112.8 113.9 %all-gather.3.cloned.1.call-done = bf16[4096,768]{0,1:T(8,128)(2,1)} async-done(((bf16[1024,768]{0,1:T(8,128)(2,1)}), bf16[4096,768]{0,1:T(8,128)(2,1)}) %all-gather.3.cloned.1.call-update) | async-done | bytes 6291472 | tf_op jit(solution)/shard_map/all_gather | solution.py:103
  226.8 34.7 %multiply_convert_fusion.1 = (bf16[4096,768]{1,0:T(8,128)(2,1)S(1)}, f32[4096,768]{1,0:T(8,128)}, f32[4096,768]{1,0:T(8,128)}) fusion(f32[768]{0:T(1024)S(1)} %convert_element_type.178, bf16[4096,768]{0,1:T(8,128)(2,1)} %all-gather.3.cloned.1.call-done, bf16[768,768]{1,0:T(8,128)(2,1)S(1)} %copy-done), kind=kOutput, calls=%fused_computation.63 | convolution fusion | flops 5039456256 | bytes 38931456 | tf_op jit(solution)/shard_map/dot_general | solution.py:17
  264.1 7.0 convolution_convert_fusion.1
  273.5 106.7 %reduce-scatter.3.cloned.1.call-done = bf16[1024,768]{0,1:T(8,128)(2,1)} async-done(((bf16[4096,768]{0,1:T(8,128)(2,1)}), bf16[1024,768]{0,1:T(8,128)(2,1)}) %reduce-scatter.3.cloned.1.call-update) | async-done | bytes 1572880 | tf_op jit(solution)/shard_map/reduce_scatter | solution.py:107
  380.2 3.2 fusion.84
  392.0 116.0 %all-gather.5.cloned.1.call-done = bf16[4096,768]{0,1:T(8,128)(2,1)} async-done(((bf16[1024,768]{0,1:T(8,128)(2,1)}), bf16[4096,768]{0,1:T(8,128)(2,1)}) %all-gather.5.cloned.1.call-update) | async-done | bytes 6291472 | tf_op jit(solution)/shard_map/all_gather | solution.py:119
  508.0 18.5 %convert_reduce_fusion = (f32[768]{0:T(1024)}, bf16[4096,768]{1,0:T(8,128)(2,1)}) fusion(f32[4096,768]{1,0:T(8,128)} %get-tuple-element.288, f32[4096,768]{1,0:T(8,128)} %get-tuple-element.296, f32[768]{0:T(1024)S(1)} %convert_element_type.178, bf16[4096,768]{0,1:T(8,128)(2,1)} %all-gather.5.cloned.1.call-done, bf16[768,768]{1,0:T(8,128)(2,1)S(1)} %copy-done.67), kind=kOutput, calls=%fused_computation.61 | convolution fusion | flops 4885314560 | bytes 38934528 | tf_op jit(solution)/shard_map/dot_general | solution.py:27
  526.5 9.7 convolution_convert_fusion
  536.5 108.9 %reduce-scatter.5.cloned.1.call-done = bf16[1024,768]{0,1:T(8,128)(2,1)} async-done(((bf16[4096,768]{0,1:T(8,128)(2,1)}), bf16[1024,768]{0,1:T(8,128)(2,1)}) %reduce-scatter.5.cloned.1.call-update) | async-done | bytes 1572880 | tf_op jit(solution)/shard_map/reduce_scatter | solution.py:125
  645.4 5.4 multiply_reduce_fusion
  662.5 3.0 copy.77
  666.8 34.0 %while.28 = (s32[]{:T(128)}, f32[256,12,64]{0,2,1:T(8,128)}, f32[256,12,64]{0,2,1:T(8,128)S(1)}, bf16[2,512,12,64]{1,3,2,0:T(8,128)(2,1)}, bf16[2,512,12,64]{1,3...) while((s32[]{:T(128)}, f32[256,12,64]{0,2,1:T(8,128)}, ...), condition=%wide.region_18.19_spmd.clone, body=%wide.region_16.18_spmd.clone.sunk | while | flops 1027270656 | bytes 112255784 | solution.py:166
  675.6 4.0 fusion.185
  679.7 4.0 fusion.186
  692.5 4.2 fusion.185
  696.7 4.0 fusion.186
  711.6 36.7 %all-reduce.15.cloned.1.call-done = (bf16[256,768]{0,1:T(8,128)(2,1)}, bf16[256,768]{0,1:T(8,128)(2,1)}) async-done(((bf16[256,768]{0,1:T(8,128)(2,1)}, bf16[256,768]{0,1:T(8,128)(2,1)}), (bf16[256,768]{0,1:T(8,128)(2,1)}, bf16[256,768]{0,1:T(8,128)(2,1)})) %all-reduce.15.cloned.1.call-update) | async-done | bytes 786448 | tf_op jit(solution)/shard_map/psum | solution.py:172
  754.0 2.9 convolution_bitcast_fusion.1
  756.8 2.9 convolution_bitcast_fusion
  764.1 10.2 fusion.92
  774.3 10.0 fusion.91
  784.3 441.6 %all-reduce.13.cloned.1.call-done = (f32[768,768]{0,1:T(8,128)}, f32[768,768]{0,1:T(8,128)}, f32[768,768]{0,1:T(8,128)}, f32[768,768]{1,0:T(8,128)}, f32[256,4096]{1,0:T(8,128)}) async-done(((f32[768,768]{0,1:T(8,128)}, f32[768,768]{0,1:T(8,128)}, f32[768,768]{0,1:T(8,128)}, f32[768,768]{1,0:T(8,128)}, f32[256,4096]{1,0:T(8,128)}), (f32[768,768]{0,1:T(8,128)}, f32[768,768]{0,1:T(8,128)}, ...) | async-done | bytes 13631504 | tf_op jit(solution)/shard_map/psum | solution.py:212
  1228.9 3.0 fusion.87
  1237.7 17.0 %all-reduce.2 = (f32[768]{0:T(1024)S(1)}, f32[768]{0:T(1024)S(1)}, f32[768]{0:T(1024)S(1)}, f32[768]{0:T(1024)S(1)}, f32[768]{0:T(1024)S(1)}, /*index=5*/f32[768...) all-reduce(f32[768]{0:T(1024)S(1)} %reduce_sum.197, ...), channel_id=1, replica_groups=mesh['dp'=8,'tp'=4] {'tp'}, use_global_device_ids=true, to_apply=%region_24.25 | all-reduce | flops 6912 | bytes 55296 | tf_op jit(solution)/shard_map/psum | solution.py:212
  1254.8 25.3 %all-reduce = (f32[768]{0:T(1024)}, f32[768]{0:T(1024)}, f32[768]{0:T(1024)}, f32[768]{0:T(1024)}, f32[768]{0:T(1024)}, /*index=5*/f32[768]{0:T(1024)}, f32[768]...) all-reduce(f32[768]{0:T(1024)S(1)} %get-tuple-element.257, ...), channel_id=1, replica_groups=mesh['dp'=8,'tp'=4] {'dp'}, use_global_device_ids=true, to_apply=%region_25.26 | all-reduce | flops 7680 | bytes 61440 | tf_op jit(solution)/shard_map/psum | solution.py:211
  1280.1 189.9 %all-reduce.11.cloned.1.call-done = (f32[768,768]{0,1:T(8,128)}, f32[768,768]{0,1:T(8,128)}, f32[768,768]{0,1:T(8,128)}, f32[768,768]{1,0:T(8,128)}, f32[256,409...) async-done(((f32[768,768]{0,1:T(8,128)}, f32[768,768]{0,1:T(8,128)}, f32[768,768]{0,1:T(8,128)}, f32[768,768]{1,0:T(8,128)}, f32[256,4096]{1,0:T(8,128)}, ...) | async-done | bytes 18350096 | tf_op jit(solution)/shard_map/psum | solution.py:211
  1470.0 3.2 copy.84
  1475.1 3.2 copy.86
  (274 shorter events, 119.6 us)
Async XLA Ops:
  7.2 219.6 %copy-start = (bf16[768,768]{1,0:T(8,128)(2,1)S(1)}, bf16[768,768]{1,0:T(8,128)(2,1)}, u32[]{:S(2)}) copy-start(bf16[768,768]{1,0:T(8,128)(2,1)} %param.38) | copy-start | bytes 3538948
  7.2 4.2 copy-start.32
  7.2 219.5 %all-gather.3.cloned.1.call-start = ((), (), s32[]{:S(2)}) async-start(), calls=%async_computation.2 | async-start | bytes 7864320 | tf_op jit(solution)/shard_map/all_gather | solution.py:103
  8.1 8.2 copy-start.46
  17.4 64.2 %copy-start.58 = (bf16[768]{0:T(1024)(128)(2,1)S(1)}, bf16[768]{0:T(1024)(128)(2,1)}, u32[]{:S(2)}) copy-start(bf16[768]{0:T(1024)(128)(2,1)} %param.28) | copy-start | bytes 4612
  102.9 4.4 copy-start.4
  102.9 4.4 copy-start.7
  102.9 4.4 copy-start.15
  102.9 4.4 copy-start.59
  102.9 4.4 copy-start.37
  102.9 4.4 copy-start.68
  112.3 267.8 %reduce-scatter.3.cloned.1.call-start = ((), (), s32[]{:S(2)}) async-start(), calls=%async_computation.3 | async-start | bytes 7864320 | tf_op jit(solution)/shard_map/reduce_scatter | solution.py:107
  112.8 151.3 %copy-start.66 = (bf16[768,768]{1,0:T(8,128)(2,1)S(1)}, bf16[768,768]{1,0:T(8,128)(2,1)}, u32[]{:S(2)}) copy-start(bf16[768,768]{1,0:T(8,128)(2,1)} %param.40) | copy-start | bytes 3538948
  271.1 236.8 %all-gather.5.cloned.1.call-start = ((), (), s32[]{:S(2)}) async-start(), calls=%async_computation.4 | async-start | bytes 7864320 | tf_op jit(solution)/shard_map/all_gather | solution.py:119
  389.9 118.1 %copy-start.67 = (bf16[768,768]{1,0:T(8,128)(2,1)S(1)}, bf16[768,768]{1,0:T(8,128)(2,1)}, u32[]{:S(2)}) copy-start(bf16[768,768]{1,0:T(8,128)(2,1)} %param.40) | copy-start | bytes 3538948
  391.9 253.4 %reduce-scatter.5.cloned.1.call-start = ((), (), s32[]{:S(2)}) async-start(), calls=%async_computation.5 | async-start | bytes 7864320 | tf_op jit(solution)/shard_map/reduce_scatter | solution.py:125
  536.3 212.0 %all-reduce.15.cloned.1.call-start = ((), (), s32[]{:S(2)}) async-start(), calls=%async_computation.8 | async-start | bytes 1572864 | tf_op jit(solution)/shard_map/psum | solution.py:172
  536.5 114.3 %copy-start.49 = (f32[1024]{0:T(1024)S(1)}, f32[1024]{0:T(1024)}, u32[]{:S(2)}) copy-start(f32[1024]{0:T(1024)} %copy-done.48) | copy-start | bytes 12292
  645.4 5.5 copy-start.10
  645.4 5.5 copy-start.14
  645.4 5.6 copy-start.26
  662.4 4.4 copy-start.5
  662.5 4.4 copy-start.8
  662.5 4.4 copy-start.16
  662.5 4.4 copy-start.44
  675.6 4.0 copy-start.12
  692.5 4.2 copy-start.12
  703.6 522.3 %all-reduce.13.cloned.1.call-start = ((), (), s32[]{:S(2)}) async-start(), calls=%async_computation.7 | async-start | bytes 27262976 | tf_op jit(solution)/shard_map/psum | solution.py:212
  708.8 39.5 %copy-start.47 = (f32[1024]{0:T(1024)S(1)}, f32[1024]{0:T(1024)}, u32[]{:S(2)}) copy-start(f32[1024]{0:T(1024)} %copy-done.46) | copy-start | bytes 12292
  750.2 6.6 copy-start.73
  763.8 706.1 %all-reduce.11.cloned.1.call-start = ((), (), s32[]{:S(2)}) async-start(), calls=%async_computation.6 | async-start | bytes 36700160 | tf_op jit(solution)/shard_map/psum | solution.py:211
  1236.1 18.7 %copy-start.56 = (f32[768]{0:T(1024)S(1)}, f32[768]{0:T(1024)}, u32[]{:S(2)}) copy-start(f32[768]{0:T(1024)} %get-tuple-element.275) | copy-start | bytes 9220
  (59 other events, 132.2 us)
Sparse Core Ops, SparseCore 0:
  112.5 114.2 all-gather.2
  271.2 108.9 reduce-scatter.2
  392.1 115.8 all-gather.4
  536.4 108.9 reduce-scatter.4
  703.7 44.5 all-reduce.14
  764.0 461.8 all-reduce.12
  1231.7 238.2 all-reduce.10
